TPU v7x, 128 devices: a whole 4x4x4 slice. The times are simulated.
128 devices in a mesh: rows: 8 (over z, x_hi), protos: 16 (over y, x_lo, core).
Axes of the slice: x: 4 (x_hi: 2, x_lo: 2; x = x_hi * 2 + x_lo), y: 4, z: 4, core: 2. Of those that a mesh axis runs over, the one named last changes fastest.
Arguments:
- teacher_rows: bfloat16 [8192, 256], P(('rows', 'protos')), may hold values from -16 to 16
- student_rows: bfloat16 [8192, 256], P(('rows', 'protos')), may hold values from -16 to 16
- prototypes: bfloat16 [256, 131072], P(None, 'protos'), may hold values from -16 to 16
Outputs:
- row_grads: float32 [8192, 256], P(('rows', 'protos'))
- row_loss: float32 [8192], P(('rows', 'protos'))
All inputs are finite; a program needn't handle non-finite values.
Results may differ from a plain program's by a relative error of at most 0.0015.
Values may be sent and summed in bfloat16 or wider, within the bound.
A program may use at most 192 MiB of HBM per device.

v0:
```python
import jax
import jax.numpy as jnp
from jax import lax
from jax.sharding import PartitionSpec as P

ITERS = 3


EPSILON = 1e-06
TEACHER_TEMP = 0.04
STUDENT_TEMP = 0.1


def unit_rows(values):
    floats = values.astype(jnp.float32)
    norms = jnp.sqrt(jnp.sum(floats * floats, axis=1, keepdims=True) + EPSILON)
    return (floats / norms, norms)


def on_device(teacher_rows, student_rows, prototypes):
    teacher_all, student_all = (
        lax.all_gather(teacher_rows, "protos", axis=0, tiled=True),
        lax.all_gather(student_rows, "protos", axis=0, tiled=True),
    )
    proto_float = prototypes.astype(jnp.float32)
    proto_norm = jnp.sqrt(jnp.sum(proto_float * proto_float, axis=0, keepdims=True) + EPSILON)
    proto_unit = proto_float / proto_norm
    proto_half = proto_unit.astype(jnp.bfloat16)
    teacher_unit = unit_rows(teacher_all)[0]
    student_unit = unit_rows(student_all)[0].astype(jnp.bfloat16)
    teacher_exp = jnp.exp(
        jnp.dot(
            teacher_unit,
            proto_unit,
            precision=lax.Precision.HIGHEST,
            preferred_element_type=jnp.float32,
        )
        / TEACHER_TEMP
    )
    student_logit = (
        jnp.dot(student_unit, proto_half, preferred_element_type=jnp.float32) / STUDENT_TEMP
    )
    student_part = jnp.sum(jnp.exp(student_logit), axis=1)
    weights = jnp.ones((teacher_exp.shape[0],), jnp.float32)
    inverse = jnp.ones((teacher_exp.shape[1],), jnp.float32)
    for sweep in range(ITERS):
        col_part = jnp.sum(teacher_exp * weights[:, None], axis=0)
        inverse = 1.0 / lax.psum(col_part, "rows")
        row_part = jnp.sum(teacher_exp * inverse[None, :], axis=1)
        row_total = lax.psum(row_part, "protos")
        weights = 1.0 / row_total
    sample_total = lax.psum(student_part, "protos")
    targets = teacher_exp * inverse[None, :] * weights[:, None]
    signal = (jnp.exp(student_logit) / sample_total[:, None] - targets).astype(jnp.bfloat16)
    loss_part = jnp.sum(targets * student_logit, axis=1)
    rows_own = student_rows.shape[0]
    offset = lax.axis_index("protos") * rows_own
    cross = lax.psum_scatter(loss_part, "protos", scatter_dimension=0, tiled=True)
    log_total = lax.dynamic_slice_in_dim(jnp.log(sample_total), offset, rows_own, 0)
    row_loss = log_total - cross
    product = (
        lax.dot_general(
            signal, proto_half, (((1,), (1,)), ((), ())), preferred_element_type=jnp.float32
        )
        / STUDENT_TEMP
    )
    summed = lax.psum(product, "protos")
    direction = lax.dynamic_slice_in_dim(summed, offset, rows_own, 0)
    own_unit, own_norm = unit_rows(student_rows)
    radial = jnp.sum(own_unit * direction, axis=1, keepdims=True)
    row_grads = (direction - own_unit * radial) / own_norm
    return (row_grads, row_loss)


def solution(mesh):
    in_specs = (P(("rows", "protos"), None), P(("rows", "protos"), None), P(None, "protos"))
    out_specs = (P(("rows", "protos"), None), P(("rows", "protos")))
    return jax.shard_map(
        on_device, mesh=mesh, in_specs=in_specs, out_specs=out_specs, check_vma=False
    )
```

profile of v0, /device:TPU:1, one launch (start us, length us, event | category | flops | bytes accessed | tf_op | source)
XLA Modules:
  0.0 553.0 jit_solution(1152270471741043094)
XLA Ops:
  7.2 3.1 fusion.1
  10.3 23.7 %all_gather.7 = bf16[1024,256]{1,0:T(8,128)(2,1)S(1)} all-gather(bf16[64,256]{1,0:T(8,128)(2,1)} %param.3), channel_id=1, replica_groups=mesh['rows'=8,'protos'=16] {'protos'}, dimensions={0}, use_global_device_ids=true | all-gather | bytes 557056 | tf_op jit(solution)/shard_map/all_gather | solution.py:22
  34.0 0.2 fusion.7
  34.2 34.5 %fusion.16 = (f32[8192]{0:T(1024)S(1)}, f32[1024,8192]{1,0:T(8,128)}) fusion(bf16[256,8192]{1,0:T(8,128)(2,1)} %param.5, f32[8192]{0:T(1024)S(1)} %add_sqrt_fusion, bf16[1024,256]{1,0:T(8,128)(2,1)S(1)} %all_gather.7, f32[1024]{0:T(1024)S(1)} %add_sqrt_fusion.1), kind=kOutput, calls=%fused_computation.43 | convolution fusion | flops 25791291392 | bytes 38342656 | tf_op jit(solution)/shard_map/dot_general | solution.py:32
  68.7 35.6 %psum.57 = f32[8192]{0:T(1024)S(1)} all-reduce(f32[8192]{0:T(1024)S(1)} %get-tuple-element.6), channel_id=1, replica_groups=mesh['rows'=8,'protos'=16] {'rows'}, use_global_device_ids=true, to_apply=%region_6.0 | all-reduce | flops 8192 | bytes 65536 | tf_op jit(solution)/shard_map/psum | solution.py:48
  104.4 12.2 %multiply_reduce_fusion.4 = f32[1024]{0:T(1024)S(1)} fusion(f32[1024,8192]{1,0:T(8,128)} %get-tuple-element.7, f32[8192]{0:T(1024)S(1)} %broadcast_divide_fusion.2), kind=kLoop, calls=%fused_computation.5 | loop fusion | flops 16776192 | bytes 33591296 | tf_op jit(solution)/shard_map/reduce_sum | solution.py:49
  116.6 33.9 %psum.58 = f32[1024]{0:T(1024)S(1)} all-reduce(f32[1024]{0:T(1024)S(1)} %multiply_reduce_fusion.4), channel_id=1, replica_groups=mesh['rows'=8,'protos'=16] {'protos'}, use_global_device_ids=true, to_apply=%region_8.0 | all-reduce | flops 1024 | bytes 8192 | tf_op jit(solution)/shard_map/psum | solution.py:50
  150.5 12.4 %multiply_reduce_fusion.3 = f32[8192]{0:T(1024)S(1)} fusion(f32[1024,8192]{1,0:T(8,128)} %get-tuple-element.7, f32[1024]{0:T(1024)S(1)} %broadcast_divide_fusion.5), kind=kLoop, calls=%fused_computation.4 | loop fusion | flops 16769024 | bytes 33591296 | tf_op jit(solution)/shard_map/reduce_sum | solution.py:47
  163.0 30.1 %psum.59 = f32[8192]{0:T(1024)S(1)} all-reduce(f32[8192]{0:T(1024)S(1)} %multiply_reduce_fusion.3), channel_id=1, replica_groups=mesh['rows'=8,'protos'=16] {'rows'}, use_global_device_ids=true, to_apply=%region_10.0 | all-reduce | flops 8192 | bytes 65536 | tf_op jit(solution)/shard_map/psum | solution.py:48
  193.1 12.2 %multiply_reduce_fusion.2 = f32[1024]{0:T(1024)S(1)} fusion(f32[1024,8192]{1,0:T(8,128)} %get-tuple-element.7, f32[8192]{0:T(1024)S(1)} %broadcast_divide_fusion.1), kind=kLoop, calls=%fused_computation.3 | loop fusion | flops 16776192 | bytes 33591296 | tf_op jit(solution)/shard_map/reduce_sum | solution.py:49
  205.3 33.9 %psum.60 = f32[1024]{0:T(1024)S(1)} all-reduce(f32[1024]{0:T(1024)S(1)} %multiply_reduce_fusion.2), channel_id=1, replica_groups=mesh['rows'=8,'protos'=16] {'protos'}, use_global_device_ids=true, to_apply=%region_12.0 | all-reduce | flops 1024 | bytes 8192 | tf_op jit(solution)/shard_map/psum | solution.py:50
  239.2 12.5 %multiply_reduce_fusion.1 = f32[8192]{0:T(1024)S(1)} fusion(f32[1024,8192]{1,0:T(8,128)} %get-tuple-element.7, f32[1024]{0:T(1024)S(1)} %broadcast_divide_fusion.4), kind=kLoop, calls=%fused_computation.2 | loop fusion | flops 16769024 | bytes 33591296 | tf_op jit(solution)/shard_map/reduce_sum | solution.py:47
  251.7 31.0 %psum.61 = f32[8192]{0:T(1024)S(1)} all-reduce(f32[8192]{0:T(1024)S(1)} %multiply_reduce_fusion.1), channel_id=1, replica_groups=mesh['rows'=8,'protos'=16] {'rows'}, use_global_device_ids=true, to_apply=%region_14.0 | all-reduce | flops 8192 | bytes 65536 | tf_op jit(solution)/shard_map/psum | solution.py:48
  282.7 12.2 %multiply_reduce_fusion.5 = f32[1024]{0:T(1024)S(1)} fusion(f32[1024,8192]{1,0:T(8,128)} %get-tuple-element.7, f32[8192]{0:T(1024)S(1)} %broadcast_divide_fusion), kind=kLoop, calls=%fused_computation.8 | loop fusion | flops 16776192 | bytes 33591296 | tf_op jit(solution)/shard_map/reduce_sum | solution.py:49
  294.9 34.1 %psum.62 = f32[1024]{0:T(1024)S(1)} all-reduce(f32[1024]{0:T(1024)S(1)} %multiply_reduce_fusion.5), channel_id=1, replica_groups=mesh['rows'=8,'protos'=16] {'protos'}, use_global_device_ids=true, to_apply=%region_16.0 | all-reduce | flops 1024 | bytes 8192 | tf_op jit(solution)/shard_map/psum | solution.py:50
  329.0 19.1 %all_gather.6 = bf16[1024,256]{1,0:T(8,128)(2,1)S(1)} all-gather(bf16[64,256]{1,0:T(8,128)(2,1)S(1)} %copy-done), channel_id=1, replica_groups=mesh['rows'=8,'protos'=16] {'protos'}, dimensions={0}, use_global_device_ids=true | all-gather | bytes 557056 | tf_op jit(solution)/shard_map/all_gather | solution.py:23
  348.3 27.3 %multiply_reduce_fusion = (f32[1024]{0:T(1024)S(1)}, f32[1024]{0:T(1024)S(1)}, f32[1024,8192]{1,0:T(8,128)}) fusion(f32[1024,8192]{1,0:T(8,128)} %get-tuple-element.7, f32[1024]{0:T(1024)S(1)} %broadcast_divide_fusion.3, f32[8192]{0:T(1024)S(1)} %broadcast_divide_fusion, bf16[256,8192]{1,0:T(8,128)(2,1)} %param.5, f32[8192]{0:T(1024)S(1)} %add_sqrt_fusion, ...), kind=kOutput, calls=%fused_computation | convolution fusion | flops 4352374784 | bytes 71909376 | tf_op jit(solution)/shard_map/dot_general | solution.py:41
  375.6 27.1 %all-reduce.1 = (f32[1024]{0:T(1024)S(1)}, f32[1024]{0:T(1024)S(1)}) all-reduce(f32[1024]{0:T(1024)S(1)} %get-tuple-element.3, f32[1024]{0:T(1024)S(1)} %get-tuple-element.2), channel_id=1, replica_groups=mesh['rows'=8,'protos'=16] {'protos'}, use_global_device_ids=true, to_apply=%region_3.0 | all-reduce | flops 2048 | bytes 16384 | tf_op jit(solution)/shard_map/psum | solution.py:52
  402.7 25.5 %fusion.4 = f32[1024,256]{1,0:T(8,128)} fusion(f32[1024,8192]{1,0:T(8,128)} %get-tuple-element.7, f32[1024,8192]{1,0:T(8,128)} %get-tuple-element.8, f32[1024]{0:T(1024)S(1)} %broadcast_divide_fusion.3, f32[8192]{0:T(1024)S(1)} %broadcast_divide_fusion, f32[1024]{0:T(1024)S(1)} %get-tuple-element.4, bf16[256,8192]{1,0:T(8,128)(2,1)} %param.5, ...), kind=kOutput, calls=%fused_computation.15 | convolution fusion | flops 4351852544 | bytes 72425472 | tf_op jit(solution)/shard_map/dot_general | solution.py:62
  428.3 0.6 dynamic-slice
  429.5 0.6 dynamic-slice_subtract_fusion
  430.2 113.3 %all-reduce.4.cloned.1.call-done = f32[1024,256]{1,0:T(8,128)} async-done(((f32[1024,256]{1,0:T(8,128)}), f32[1024,256]{1,0:T(8,128)}) %all-reduce.4.cloned.1.call-update) | async-done | bytes 1048592 | tf_op jit(solution)/shard_map/psum | solution.py:67
  543.5 1.0 multiply_reduce_fusion.6
  544.6 1.6 subtract_divide_fusion
  (19 shorter events, 0.5 us)
Async XLA Ops:
  7.2 536.4 %all-reduce.4.cloned.1.call-start = ((), (), s32[]{:S(2)}) async-start(), calls=%async_computation | async-start | bytes 2097152 | tf_op jit(solution)/shard_map/psum | solution.py:67
  239.2 89.8 %copy-start = (bf16[64,256]{1,0:T(8,128)(2,1)S(1)}, bf16[64,256]{1,0:T(8,128)(2,1)}, u32[]{:S(2)}) copy-start(bf16[64,256]{1,0:T(8,128)(2,1)} %param.4) | copy-start | bytes 98308
  402.7 25.5 %copy-start.1 = (u32[128]{0:T(128)S(1)}, u32[128]{0:T(128)}, u32[]{:S(2)}) copy-start(u32[128]{0:T(128)} %constant.31) | copy-start | bytes 1540
Sparse Core Ops, SparseCore 0:
  428.4 115.1 all-reduce.3
where the time goes:
time: 554 us; the launch traced here: 553 us
  blocking collectives  269 us (49%)
  waiting for transfers between devices  113 us (20%)
  matrix products  87.3 us (16%)
  other arithmetic  68.4 us (12%)
  between operations  14.8 us (3%)
    psum x1, waiting for transfers between devices, on_device(): summed = lax.psum(product, 'protos')  113 us
    psum x3, blocking collectives, on_device(): row_total = lax.psum(row_part, 'protos')  102 us
    psum x3, blocking collectives, on_device(): inverse = 1.0 / lax.psum(col_part, 'rows')  96.8 us
    reduce_sum x3, other arithmetic, on_device(): row_part = jnp.sum(teacher_exp * inverse[None, :], axis=1)  36.6 us
    dot_general x1, matrix products, on_device(): jnp.dot(teacher_unit, proto_unit, precision=lax.Precision.HIGHEST, prefer...  34.5 us
    dot_general x1, matrix products, on_device(): jnp.dot(student_unit, proto_half, preferred_element_type=jnp.float32)  27.3 us
    psum x1, blocking collectives, on_device(): sample_total = lax.psum(student_part, 'protos')  27.1 us
    dot_general x1, matrix products, on_device(): lax.dot_general(signal, proto_half, (((1,), (1,)), ((), ())), preferred_e...  25.5 us
  transfers between devices with their start and end apart: 1, of which 1 were waited for; matrix products, arithmetic and copies ran while one was open for 0% of the time, Pallas kernels for 0%

commit v1 on v0

v1 whole, which is shorter than its diff:
```python
import functools
import math

import jax
import jax.numpy as jnp
from jax import lax
from jax.experimental import pallas as pl
from jax.experimental.pallas import tpu as pltpu
from jax.sharding import PartitionSpec as P

ITERS = 3
EPSILON = 1e-06
TEACHER_TEMP = 0.04
STUDENT_TEMP = 0.1
LOG2E = math.log2(math.e)

R = 8
NP = 16
Y = 4
OWN = 64
PLANE = 256
ROWS = 1024
D = 256
K = 8192
LANES = 128
NCH = 4
CW = K // NCH
CT = CW // LANES
KT = K // LANES
KE = 1024
MESH = pl.DeviceIdType.MESH
NT = (((1,), (1,)), ((), ()))


def kernel(
    tea_hbm, stu_hbm, pro_hbm,
    grad_ref, loss_ref,
    exps, proto, half, tea, stu, unit,
    tscale, wexp, racc, sacc, own_buf,
    rnorm, invb, colp, colr, rowr,
    ga, gb, pxa, pxb, psa, psb, rsa, rsb, tota, totb,
    load_sem, g_send, g_recv, c_send, c_recv, r_send, r_recv,
    t_send, t_recv, p_send, p_recv, s_send, s_recv,
):
    r = lax.axis_index("rows")
    p = lax.axis_index("protos")
    y, x, c = p // 4, (p // 2) % 2, p % 2
    pc = 1 - c

    def pidx(yy, xx, cc):
        return yy * 4 + xx * 2 + cc

    def slot(yy, xx, cc):
        return yy * 4 + cc * 2 + xx

    partner = pidx(y, x, pc)
    my_slot = slot(y, x, c)

    def rcopy(src, dst, ssem, rsem, rr, pp):
        return pltpu.make_async_remote_copy(
            src_ref=src, dst_ref=dst, send_sem=ssem, recv_sem=rsem,
            device_id=(rr, pp), device_id_type=MESH,
        )

    barrier = pltpu.get_barrier_semaphore()
    for j in range(1, R):
        pl.semaphore_signal(barrier, inc=1, device_id=((r + j) % R, p), device_id_type=MESH)
    for j in range(1, NP):
        pl.semaphore_signal(barrier, inc=1, device_id=(r, (p + j) % NP), device_id_type=MESH)
    loads = (
        pltpu.make_async_copy(tea_hbm, tea.at[my_slot], load_sem.at[0]),
        pltpu.make_async_copy(stu_hbm, stu.at[my_slot], load_sem.at[1]),
        pltpu.make_async_copy(pro_hbm, proto, load_sem.at[2]),
    )
    for copy in loads:
        copy.start()
    loads[0].wait()
    loads[1].wait()
    pl.semaphore_wait(barrier, R - 1 + NP - 1)

    sends = []

    def start(copy):
        copy.start()
        sends.append(copy)

    peers = [(dy, dx) for dy in (1, 3, 0, 2) for dx in (0, 1) if (dy, dx) != (0, 0)]
    peers.sort(key=lambda q: ((0, 1, 2, 1)[q[0]] + q[1]))
    bufs = (tea, stu)

    def gather_start(a):
        buf = bufs[a]
        mine = buf.at[my_slot]
        start(rcopy(mine, mine, g_send.at[a, 0], g_recv.at[a, my_slot], r, partner))
        for dy, dx in peers:
            start(rcopy(mine, mine, g_send.at[a, 1 + dy * 2 + dx], g_recv.at[a, my_slot],
                        r, pidx((y + dy) % Y, (x + dx) % 2, c)))

    def gather_wait(a, q):
        block = bufs[a].at[q]
        rcopy(block, block, g_send.at[a, 0], g_recv.at[a, q], r, partner).wait_recv()

    def gather_direct(a, dy):
        ys = (y + dy) % Y
        for dx in (0, 1):
            if (dy, dx) == (0, 0):
                continue
            q = slot(ys, (x + dx) % 2, c)
            gather_wait(a, q)
            block = bufs[a].at[q]
            start(rcopy(block, block, g_send.at[a, 8 + dy * 2 + dx], g_recv.at[a, q], r, partner))

    def gather_passed(a, dy):
        ys = (y + dy) % Y
        for dx in (0, 1):
            gather_wait(a, slot(ys, dx, pc))

    gather_start(0)
    gather_start(1)

    loads[2].wait()

    def norm_step(t, carry):
        cols = pl.ds(pl.multiple_of(t * 256, 256), 256)
        v = proto[:, cols].astype(jnp.float32)
        total = jnp.sum(v * v, axis=0, keepdims=True)
        rnorm[:, cols] = jnp.broadcast_to(1.0 / jnp.sqrt(total + EPSILON), (8, 256))
        return carry

    lax.fori_loop(0, K // 256, norm_step, 0)

    def column_send(it, ch):
        piece = pl.ds(ch * CT, CT)
        mine = colr.at[it, r, piece]
        for j in range(1, R):
            start(rcopy(mine, mine, c_send.at[it, ch, j], c_recv.at[it, ch, r], (r + j) % R, p))

    def column_wait(it, ch):
        piece = pl.ds(ch * CT, CT)
        for j in range(1, R):
            rr = (r + j) % R
            theirs = colr.at[it, rr, piece]
            rcopy(theirs, theirs, c_send.at[it, ch, j], c_recv.at[it, ch, rr], rr, p).wait_recv()
        total = colr[it, 0, piece]
        for j in range(1, R):
            total = total + colr[it, j, piece]
        inverse = 1.0 / total
        for t in range(CT):
            invb[:, pl.ds(ch * CW + t * LANES, LANES)] = jnp.broadcast_to(
                inverse[t : t + 1, :], (8, LANES)
            )

    order = (0, 1, 3, 2)
    for s in range(4):
        if s == 0:
            gather_direct(0, order[0])
        if s < 3:
            gather_direct(0, order[s + 1])
        gather_passed(0, order[s])
        ys = (y + order[s]) % Y
        row0 = pl.multiple_of(ys * PLANE, PLANE)
        rows = pl.ds(row0, PLANE)
        plane = tea[pl.ds(ys * 4, 4)].reshape(PLANE, D)
        wide = plane.astype(jnp.float32)
        total = jnp.sum(wide * wide, axis=1, keepdims=True)
        scale = (LOG2E / TEACHER_TEMP) / jnp.sqrt(total + EPSILON)
        tscale[rows, :] = jnp.broadcast_to(scale, (PLANE, LANES))

        def exp_step(t, carry, s=s, ys=ys, rows=rows):
            cols = pl.ds(pl.multiple_of(t * KE, KE), KE)
            block = tea[pl.ds(ys * 4, 4)].reshape(PLANE, D)
            dots = jnp.dot(block, proto[:, cols], preferred_element_type=jnp.float32)
            rn = rnorm[:, cols]
            row_scale = tscale[rows, :].reshape(PLANE // 8, 8, LANES)
            for j in range(KE // LANES):
                part = dots[:, j * LANES : (j + 1) * LANES].reshape(PLANE // 8, 8, LANES)
                value = jnp.exp2(part * row_scale * rn[None, :, j * LANES : (j + 1) * LANES])
                where = pl.ds(pl.multiple_of(t * KE + j * LANES, LANES), LANES)
                exps[rows, where] = value.reshape(PLANE, LANES)
                added = jnp.sum(value, axis=0)
                if s == 0:
                    colp[:, where] = added
                else:
                    colp[:, where] = colp[:, where] + added
            return carry

        if s < 3:
            lax.fori_loop(0, K // KE, exp_step, 0)
        else:
            for ch in range(NCH):
                lax.fori_loop(ch * CW // KE, (ch + 1) * CW // KE, exp_step, 0)
                for t in range(CT):
                    k = ch * CT + t
                    colr[0, r, k : k + 1, :] = jnp.sum(
                        colp[:, k * LANES : (k + 1) * LANES], axis=0, keepdims=True
                    )
                column_send(0, ch)

    for dy in order:
        gather_direct(1, dy)

    def half_step(t, carry):
        cols = pl.ds(pl.multiple_of(t * 256, 256), 256)
        rn = jnp.broadcast_to(rnorm[0:1, cols], (D, 256))
        half[:, cols] = (proto[:, cols].astype(jnp.float32) * rn).astype(jnp.bfloat16)
        return carry

    lax.fori_loop(0, K // 256, half_step, 0)
    for dy in order:
        gather_passed(1, dy)

    def unit_step(t, carry):
        wide = stu[t].astype(jnp.float32)
        total = jnp.sum(wide * wide, axis=1, keepdims=True)
        unit[pl.ds(pl.multiple_of(t * OWN, OWN), OWN), :] = (
            wide / jnp.sqrt(total + EPSILON)
        ).astype(jnp.bfloat16)
        return carry

    lax.fori_loop(0, NP, unit_step, 0)

    def student_piece(k):
        cols = pl.ds(k * KE, KE)

        def step(b, carry):
            rows = pl.ds(pl.multiple_of(b * PLANE, PLANE), PLANE)
            logits = jnp.dot(unit[rows, :], half[:, cols], preferred_element_type=jnp.float32)
            value = jnp.exp2(logits * (LOG2E / STUDENT_TEMP))
            total = value[:, :LANES]
            for j in range(1, KE // LANES):
                total = total + value[:, j * LANES : (j + 1) * LANES]
            product = lax.dot_general(
                value.astype(jnp.bfloat16), half[:, cols], NT, preferred_element_type=jnp.float32
            )
            if k == 0:
                sacc[rows, :] = total
                ga[rows, :] = product
            else:
                sacc[rows, :] = sacc[rows, :] + total
                ga[rows, :] = ga[rows, :] + product
            return carry

        lax.fori_loop(0, ROWS // PLANE, step, 0)

    def row_pass(ch):
        def step(g, carry):
            rows = pl.ds(pl.multiple_of(g * 64, 64), 64)
            acc = jnp.zeros((8, 8, LANES), jnp.float32)
            if ch > 0:
                acc = racc[rows, :].reshape(8, 8, LANES)
            for j in range(CT):
                where = pl.ds(ch * CW + j * LANES, LANES)
                acc = acc + exps[rows, where].reshape(8, 8, LANES) * invb[:, where][None]
            racc[rows, :] = acc.reshape(64, LANES)
            return carry

        lax.fori_loop(0, ROWS // 64, step, 0)

    def row_send(it):
        for t in range(8):
            rowr[it, my_slot, t : t + 1, :] = jnp.sum(
                racc[t * LANES : (t + 1) * LANES, :].T, axis=0, keepdims=True
            )
        mine = rowr.at[it, my_slot]
        for j in range(1, NP):
            start(rcopy(mine, mine, r_send.at[it, j], r_recv.at[it, my_slot], r, (p + j) % NP))

    def row_wait(it):
        for j in range(1, NP):
            q = (p + j) % NP
            theirs = rowr.at[it, slot(q // 4, (q // 2) % 2, q % 2)]
            rcopy(theirs, theirs, r_send.at[it, j],
                  r_recv.at[it, slot(q // 4, (q // 2) % 2, q % 2)], r, q).wait_recv()
        total = rowr[it, 0]
        for j in range(1, NP):
            total = total + rowr[it, j]
        weights = 1.0 / total
        for t in range(8):
            wexp[t * LANES : (t + 1) * LANES, :] = jnp.broadcast_to(
                weights[t : t + 1, :], (LANES, LANES)
            ).T

    def column_pass(it, ch):
        for h in range(CW // 1024):
            def step(g, accs, h=h):
                rows = pl.ds(pl.multiple_of(g * 64, 64), 64)
                w = wexp[rows, :].reshape(8, 8, LANES)
                out = []
                for j in range(8):
                    where = pl.ds(ch * CW + h * 1024 + j * LANES, LANES)
                    part = exps[rows, where].reshape(8, 8, LANES) * w
                    out.append(accs[j] + jnp.sum(part, axis=0))
                return tuple(out)

            accs = lax.fori_loop(
                0, ROWS // 64, step, tuple(jnp.zeros((8, LANES), jnp.float32) for _ in range(8))
            )
            for j in range(8):
                k = ch * CT + h * 8 + j
                colr[it, r, k : k + 1, :] = jnp.sum(accs[j], axis=0, keepdims=True)
        column_send(it, ch)

    def owner_send(kind, acc, buf, dy):
        ys = (y + dy) % Y
        for t in range(2):
            block = acc[pl.ds(pl.multiple_of(ys * PLANE + t * LANES, LANES), LANES), :]
            buf[ys, my_slot, t : t + 1, :] = jnp.sum(block.T, axis=0, keepdims=True)
        mine = buf.at[ys, my_slot]
        for dx in (0, 1):
            for dc in (0, 1):
                if (dy, dx, dc) == (0, 0, 0):
                    continue
                q = pidx(ys, (x + dx) % 2, (c + dc) % 2)
                start(rcopy(mine, mine, t_send.at[kind, dy * 4 + dx * 2 + dc],
                            t_recv.at[kind, my_slot], r, q))

    def owner_total(kind, buf):
        for j in range(1, NP):
            q = (p + j) % NP
            their = slot(q // 4, (q // 2) % 2, q % 2)
            block = buf.at[y, their]
            rcopy(block, block, t_send.at[kind, j], t_recv.at[kind, their], r, q).wait_recv()
        total = buf[y, 0]
        for j in range(1, NP):
            total = total + buf[y, j]
        for t in range(2):
            own_buf[kind, t * LANES : (t + 1) * LANES, :] = jnp.broadcast_to(
                total[t : t + 1, :], (LANES, LANES)
            ).T
        return own_buf[kind, pl.ds(pl.multiple_of(c * LANES + x * OWN, OWN), OWN), :]

    def pair_copy(kind, g, px, dy):
        ys = (y + dy) % Y
        rows = pl.ds(pl.multiple_of(ys * PLANE + pc * LANES, LANES), LANES)
        return rcopy(g.at[rows], px.at[ys], p_send.at[kind, dy], p_recv.at[kind, dy], r, partner)

    def scatter_send(kind, g, px, ps, rs, dy):
        ys = (y + dy) % Y
        block = px.at[ys]
        rcopy(block, block, p_send.at[kind, dy], p_recv.at[kind, dy], r, partner).wait_recv()
        rows = pl.ds(pl.multiple_of(ys * PLANE + c * LANES, LANES), LANES)
        ps[ys] = g[rows, :] + px[ys]
        for dx in (0, 1):
            if (dy, dx) == (0, 0):
                continue
            xs = (x + dx) % 2
            src = ps.at[ys, pl.ds(pl.multiple_of(xs * OWN, OWN), OWN)]
            start(rcopy(src, rs.at[y * 2 + x], s_send.at[kind, dy * 2 + dx],
                        s_recv.at[kind, y * 2 + x], r, pidx(ys, xs, c)))

    def scatter_total(kind, ps, rs):
        total = ps[y, pl.ds(pl.multiple_of(x * OWN, OWN), OWN), :]
        for dy, dx in peers:
            q = ((y + dy) % Y) * 2 + (x + dx) % 2
            block = rs.at[q]
            rcopy(block, block, s_send.at[kind, dy * 2 + dx], s_recv.at[kind, q], r,
                  partner).wait_recv()
            total = total + rs[q]
        return total

    far_first = (2, 1, 3, 0)

    for k in (0, 1):
        student_piece(k)
    for ch in range(NCH):
        column_wait(0, ch)
        row_pass(ch)
    row_send(0)
    for k in (2, 3, 4):
        student_piece(k)
    row_wait(0)
    for ch in range(NCH):
        column_pass(1, ch)
    for k in (5, 6, 7):
        student_piece(k)
    for ch in range(NCH):
        column_wait(1, ch)
        row_pass(ch)
    row_send(1)
    for dy in far_first:
        start(pair_copy(0, ga, pxa, dy))
    row_wait(1)
    for ch in range(NCH):
        column_pass(2, ch)
        scatter_send(0, ga, pxa, psa, rsa, far_first[ch])
    for dy in far_first:
        owner_send(0, sacc, tota, dy)

    for i, dy in enumerate(far_first):
        ys = (y + dy) % Y
        rows = pl.ds(pl.multiple_of(ys * PLANE, PLANE), PLANE)
        for ch in range(NCH):
            if i == 0:
                column_wait(2, ch)

            def step(t, carry, rows=rows):
                cols = pl.ds(pl.multiple_of(t * KE, KE), KE)
                value = exps[rows, cols].reshape(PLANE // 8, 8, KE) * invb[:, cols][None]
                value = value.reshape(PLANE, KE)
                total = value[:, :LANES]
                for j in range(1, KE // LANES):
                    total = total + value[:, j * LANES : (j + 1) * LANES]
                product = lax.dot_general(
                    value.astype(jnp.bfloat16), half[:, cols], NT,
                    preferred_element_type=jnp.float32,
                )
                racc[rows, :] = racc[rows, :] + total
                gb[rows, :] = gb[rows, :] + product
                return carry

            if ch == 0:
                racc[rows, :] = jnp.zeros((PLANE, LANES), jnp.float32)
                gb[rows, :] = jnp.zeros((PLANE, D), jnp.float32)
            lax.fori_loop(ch * CW // KE, (ch + 1) * CW // KE, step, 0)
        start(pair_copy(1, gb, pxb, dy))
        owner_send(1, racc, totb, dy)
        if i > 0:
            scatter_send(1, gb, pxb, psb, rsb, far_first[i - 1])
    scatter_send(1, gb, pxb, psb, rsb, far_first[3])

    sample_total = owner_total(0, tota)
    first = scatter_total(0, psa, rsa)
    row_total = owner_total(1, totb)
    second = scatter_total(1, psb, rsb)
    weight = 1.0 / row_total
    inv_sample = 1.0 / sample_total
    wide_s = jnp.concatenate([inv_sample, inv_sample], axis=1)
    wide_w = jnp.concatenate([weight, weight], axis=1)
    pulled = second * wide_w
    direction = (first * wide_s - pulled) / STUDENT_TEMP
    floats = stu[my_slot].astype(jnp.float32)
    norm = jnp.sqrt(jnp.sum(floats * floats, axis=1, keepdims=True) + EPSILON)
    own = floats / norm
    half_own = own.astype(jnp.bfloat16).astype(jnp.float32)
    cross = jnp.sum(half_own * pulled, axis=1, keepdims=True) / STUDENT_TEMP
    radial = jnp.sum(own * direction, axis=1, keepdims=True)
    grad_ref[...] = (direction - own * radial) / norm
    loss_ref[...] = jnp.log(sample_total) - jnp.broadcast_to(cross, (OWN, LANES))
    for copy in sends:
        copy.wait_send()


def on_device(teacher_rows, student_rows, prototypes):
    f32, bf16 = jnp.float32, jnp.bfloat16
    vmem = lambda shape, dtype=f32: pltpu.VMEM(shape, dtype)
    dma = lambda *shape: pltpu.SemaphoreType.DMA(shape)
    grads, loss = pl.pallas_call(
        kernel,
        out_shape=(
            jax.ShapeDtypeStruct((OWN, D), f32),
            jax.ShapeDtypeStruct((OWN, LANES), f32),
        ),
        in_specs=[pl.BlockSpec(memory_space=pl.ANY)] * 3,
        out_specs=(pl.BlockSpec(memory_space=pltpu.VMEM), pl.BlockSpec(memory_space=pltpu.VMEM)),
        scratch_shapes=[
            vmem((ROWS, K)),
            vmem((D, K), bf16), vmem((D, K), bf16),
            vmem((NP, OWN, D), bf16), vmem((NP, OWN, D), bf16),
            vmem((ROWS, D), bf16),
            vmem((ROWS, LANES)), vmem((ROWS, LANES)),
            vmem((ROWS, LANES)), vmem((ROWS, LANES)),
            vmem((2, PLANE, LANES)),
            vmem((8, K)), vmem((8, K)), vmem((8, K)),
            vmem((ITERS, R, KT, LANES)),
            vmem((2, NP, 8, LANES)),
            vmem((ROWS, D)), vmem((ROWS, D)),
            vmem((Y, LANES, D)), vmem((Y, LANES, D)),
            vmem((Y, LANES, D)), vmem((Y, LANES, D)),
            vmem((8, OWN, D)), vmem((8, OWN, D)),
            vmem((Y, NP, 2, LANES)), vmem((Y, NP, 2, LANES)),
            dma(3),
            dma(2, 16), dma(2, NP),
            dma(ITERS, NCH, R), dma(ITERS, NCH, R),
            dma(2, NP), dma(2, NP),
            dma(2, NP), dma(2, NP),
            dma(2, Y), dma(2, Y),
            dma(2, 8), dma(2, 8),
        ],
        compiler_params=pltpu.CompilerParams(
            collective_id=0, has_side_effects=True, vmem_limit_bytes=67043328
        ),
        name="prototype_head",
    )(teacher_rows, student_rows, prototypes)
    return grads, loss[:, 0]


def solution(mesh):
    in_specs = (P(("rows", "protos"), None), P(("rows", "protos"), None), P(None, "protos"))
    out_specs = (P(("rows", "protos"), None), P(("rows", "protos")))
    return jax.shard_map(
        on_device, mesh=mesh, in_specs=in_specs, out_specs=out_specs, check_vma=False
    )
```

time: 554 us -> 98.7 us (0.18)
  blocking collectives: 269 us -> 0 us
  waiting for transfers between devices: 113 us -> 0 us
  Pallas kernels: 0 us -> 95 us
  matrix products: 87.3 us -> 0 us
  other arithmetic: 68.4 us -> 0 us
  between operations: 14.8 us -> 0.64 us
    psum x7 -> x0, blocking collectives: 226 us -> none  [the longest x3 102 us: on_device(): row_total = lax.psum(row_part, 'protos')]
    psum x1 -> x0, waiting for transfers between devices: 113 us -> none  [on_device(): summed = lax.psum(product, 'protos')]
    pallas_call x0 -> x1, Pallas kernels: none -> 95 us  [on_device(): pl.pallas_call(kernel, out_shape=(jax.ShapeDtypeStruct((OWN, D), f32), ja...]
    dot_general x3 -> x0, matrix products: 87.3 us -> none  [the longest x1 34.5 us: on_device(): jnp.dot(teacher_unit, proto_unit, precision=lax.Precision.HIGHEST, prefer...]
    reduce_sum x10 -> x0, other arithmetic: 66.1 us -> none  [the longest x3 36.6 us: on_device(): row_part = jnp.sum(teacher_exp * inverse[None, :], axis=1)]
    all_gather x2 -> x0, blocking collectives: 42.7 us -> none  [the longest x1 23.7 us: on_device(): lax.all_gather(teacher_rows, 'protos', axis=0, tiled=True)]
  transfers between devices with their start and end apart: 1 -> 0, of which waited for: 1 -> 0; matrix products, arithmetic and copies ran while one was open for 0% -> 0% of each run, Pallas kernels for 0% -> 0%
where the time goes in v1:
time: 98.7 us; the launch traced here: 98.5 us
  Pallas kernels  95 us (96%)
  local copies, waits for them, and re-layouts  2.86 us (3%)
    pallas_call x1, Pallas kernels, on_device(): pl.pallas_call(kernel, out_shape=(jax.ShapeDtypeStruct((OWN, D), f32), ja...  95 us

profile of v1, /device:TPU:1, one launch (start us, length us, event | category | flops | bytes accessed | tf_op | source)
XLA Modules:
  0.0 98.5 jit_solution(10489247802937480611)
XLA Ops:
  0.6 95.0 %prototype_head.1 = (f32[64,256]{1,0:T(8,128)}, f32[64,128]{1,0:T(8,128)}) custom-call(bf16[64,256]{1,0:T(8,128)(2,1)} %tea_hbm.1, bf16[64,256]{1,0:T(8,128)(2,1)} %stu_hbm.1, bf16[256,8192]{1,0:T(8,128)(2,1)} %pro_hbm.1), custom_call_target="tpu_custom_call" | custom-call | tf_op jit(solution)/shard_map/prototype_head/pallas_call | solution.py:447
  95.6 1.4 %slice_reduce_fusion = f32[64]{0:T(128)} fusion(f32[64,128]{1,0:T(8,128)} %get-tuple-element.5), kind=kLoop, calls=%fused_computation | loop fusion | bytes 512 | tf_op jit(solution)/shard_map/slice | solution.py:484
  97.0 1.5 %copy.6 = f32[64,256]{1,0:T(8,128)} copy(f32[64,256]{1,0:T(8,128)} %get-tuple-element.8) | data formatting | bytes 131072

commit v2 on v1

v2 whole, which is shorter than its diff:
```python
import contextlib
import math

import jax
import jax.numpy as jnp
from jax import lax
from jax.experimental import pallas as pl
from jax.experimental.pallas import tpu as pltpu
from jax.sharding import PartitionSpec as P

ITERS = 3
EPSILON = 1e-06
TEACHER_TEMP = 0.04
STUDENT_TEMP = 0.1
LOG2E = math.log2(math.e)

R = 8
NP = 16
Y = 4
OWN = 64
PLANE = 256
ROWS = 1024
D = 256
K = 8192
LANES = 128
NCH = 4
CW = K // NCH
CT = CW // LANES
RB = 256
KT = K // LANES
MESH = pl.DeviceIdType.MESH
scope = lambda name: contextlib.nullcontext()
NT = (((1,), (1,)), ((), ()))


def kernel(
    tea_hbm, stu_hbm, pro_hbm,
    grad_ref, loss_ref,
    exps, proto, half, tea, stu, unit,
    tscale, wexp, racc, sacc, own_buf,
    rnorm, invb, colp, colr, rowr,
    ga, gb, pxa, pxb, psa, psb, rsa, rsb, tota, totb, ownd, owns,
    load_sem, g_send, g_recv, c_send, c_recv, r_send, r_recv,
    t_send, t_recv, p_send, p_recv, s_send, s_recv,
):
    r = lax.axis_index("rows")
    p = lax.axis_index("protos")
    y, x, c = p // 4, (p // 2) % 2, p % 2
    pc = 1 - c

    def pidx(yy, xx, cc):
        return yy * 4 + xx * 2 + cc

    def slot(yy, xx, cc):
        return yy * 4 + cc * 2 + xx

    partner = pidx(y, x, pc)
    my_slot = slot(y, x, c)

    def rcopy(src, dst, ssem, rsem, rr, pp):
        return pltpu.make_async_remote_copy(
            src_ref=src, dst_ref=dst, send_sem=ssem, recv_sem=rsem,
            device_id=(rr, pp), device_id_type=MESH,
        )

    barrier = pltpu.get_barrier_semaphore()
    for j in range(1, R):
        pl.semaphore_signal(barrier, inc=1, device_id=((r + j) % R, p), device_id_type=MESH)
    for j in range(1, NP):
        pl.semaphore_signal(barrier, inc=1, device_id=(r, (p + j) % NP), device_id_type=MESH)
    loads = (
        pltpu.make_async_copy(tea_hbm, tea.at[my_slot], load_sem.at[0]),
        pltpu.make_async_copy(stu_hbm, stu.at[my_slot], load_sem.at[1]),
        pltpu.make_async_copy(pro_hbm, proto, load_sem.at[2]),
    )
    for copy in loads:
        copy.start()
    loads[0].wait()
    loads[1].wait()
    pl.semaphore_wait(barrier, R - 1 + NP - 1)

    peers = [(0, 1), (1, 0), (3, 0), (1, 1), (3, 1), (2, 0), (2, 1)]
    bufs = (tea, stu)

    def gather_start(a):
        mine = bufs[a].at[my_slot]
        rcopy(mine, mine, g_send.at[a], g_recv.at[a, 1, y], r, partner).start()
        for dy, dx in peers:
            rcopy(mine, mine, g_send.at[a], g_recv.at[a, 0, y],
                  r, pidx((y + dy) % Y, (x + dx) % 2, c)).start()

    def gather_direct(a, dy):
        ys = (y + dy) % Y
        if dy == 0:
            blocks = bufs[a].at[pl.ds(slot(y, 1 - x, c), 1)]
        else:
            blocks = bufs[a].at[pl.ds(slot(ys, 0, c), 2)]
        rcopy(blocks, blocks, g_send.at[a], g_recv.at[a, 0, ys], r, partner).wait_recv()
        for dx in (0, 1):
            if (dy, dx) != (0, 0):
                block = bufs[a].at[slot(ys, (x + dx) % 2, c)]
                rcopy(block, block, g_send.at[a], g_recv.at[a, 1, ys], r, partner).start()

    def gather_passed(a, dy):
        ys = (y + dy) % Y
        blocks = bufs[a].at[pl.ds(slot(ys, 0, pc), 2)]
        rcopy(blocks, blocks, g_send.at[a], g_recv.at[a, 1, ys], r, partner).wait_recv()

    with scope("gather_start"):
        gather_start(0)

    loads[2].wait()

    def norm_step(t, carry):
        cols = pl.ds(pl.multiple_of(t * 512, 512), 512)
        v = proto[:, cols].astype(jnp.float32)
        total = jnp.sum(v * v, axis=0, keepdims=True)
        inverse = 1.0 / jnp.sqrt(total + EPSILON)
        rnorm[:, cols] = jnp.broadcast_to(inverse, (8, 512))
        half[:, cols] = (v * inverse).astype(jnp.bfloat16)
        return carry

    with scope("norms"):
        lax.fori_loop(0, K // 512, norm_step, 0)

    def column_send(it, ch):
        piece = pl.ds(ch * CT, CT)
        mine = colr.at[it, r, piece]
        for j in range(1, R):
            rcopy(mine, mine, c_send, c_recv.at[it, ch], (r + j) % R, p).start()

    def column_wait(it, ch):
        piece = pl.ds(ch * CT, CT)
        theirs = colr.at[it, pl.ds(0, R - 1), piece]
        rcopy(theirs, theirs, c_send, c_recv.at[it, ch], r, p).wait_recv()
        total = colr[it, 0, piece]
        for j in range(1, R):
            total = total + colr[it, j, piece]
        inverse = 1.0 / total
        for t in range(CT):
            invb[ch * CT + t] = jnp.broadcast_to(inverse[t : t + 1, :], (8, LANES))

    order = (0, 1, 3, 2)

    def exp_tiles(rows, block, first, k0, k1):
        dots = jnp.dot(
            block, proto[:, k0 * LANES : k1 * LANES], preferred_element_type=jnp.float32
        )
        row_scale = tscale[rows, :].reshape(PLANE // 8, 8, LANES)
        for k in range(k0, k1):
            part = dots[:, (k - k0) * LANES : (k - k0 + 1) * LANES]
            part = part.reshape(PLANE // 8, 8, LANES)
            value = jnp.exp2(part * row_scale * rnorm[:, k * LANES : (k + 1) * LANES][None])
            exps[k, rows, :] = value.reshape(PLANE, LANES)
            added = jnp.sum(value, axis=0)
            colp[k] = added if first else colp[k] + added

    for s in range(4):
        with scope("gather_wait"):
            if s == 0:
                gather_direct(0, order[0])
            if s < 3:
                gather_direct(0, order[s + 1])
            gather_passed(0, order[s])
        if s == 0:
            gather_start(1)
        with scope("exp_plane"):
            ys = (y + order[s]) % Y
            rows = pl.ds(pl.multiple_of(ys * PLANE, PLANE), PLANE)
            block = tea[pl.ds(ys * 4, 4)].reshape(PLANE, D)
            wide = block.astype(jnp.float32)
            total = jnp.sum(wide * wide, axis=1, keepdims=True)
            scale = (LOG2E / TEACHER_TEMP) / jnp.sqrt(total + EPSILON)
            tscale[rows, :] = jnp.broadcast_to(scale, (PLANE, LANES))
            if s < 3:
                exp_tiles(rows, block, s == 0, 0, KT)
            else:
                for h in range(2):
                    exp_tiles(rows, block, False, h * KT // 2, (h + 1) * KT // 2)
                    for ch in range(h * NCH // 2, (h + 1) * NCH // 2):
                        for k in range(ch * CT, (ch + 1) * CT):
                            colr[0, r, k : k + 1, :] = jnp.sum(colp[k], axis=0, keepdims=True)
                        column_send(0, ch)

    with scope("student_rows"):
        for dy in order:
            gather_direct(1, dy)
        for dy in order:
            gather_passed(1, dy)

        def unit_step(t, carry):
            wide = stu[pl.ds(t * 4, 4)].reshape(PLANE, D).astype(jnp.float32)
            total = jnp.sum(wide * wide, axis=1, keepdims=True)
            unit[pl.ds(pl.multiple_of(t * PLANE, PLANE), PLANE), :] = (
                wide / jnp.sqrt(total + EPSILON)
            ).astype(jnp.bfloat16)
            return carry

        lax.fori_loop(0, Y, unit_step, 0)

    def student_piece(dy):
        ys = (y + dy) % Y
        rows = pl.ds(pl.multiple_of(ys * PLANE, PLANE), PLANE)
        logits = jnp.dot(unit[rows, :], half[...], preferred_element_type=jnp.float32)
        value = jnp.exp2(logits * (LOG2E / STUDENT_TEMP))
        total = value[:, :LANES]
        for k in range(1, KT):
            total = total + value[:, k * LANES : (k + 1) * LANES]
        sacc[rows, :] = total
        ga[rows, :] = lax.dot_general(
            value.astype(jnp.bfloat16), half[...], NT, preferred_element_type=jnp.float32
        )
        pair_copy(0, ga, pxa, dy).start()

    def row_pass(ch):
        def step(g, carry):
            rows = pl.ds(pl.multiple_of(g * RB, RB), RB)
            acc = jnp.zeros((RB // 8, 8, LANES), jnp.float32)
            if ch > 0:
                acc = racc[rows, :].reshape(RB // 8, 8, LANES)
            for k in range(ch * CT, (ch + 1) * CT):
                acc = acc + exps[k, rows, :].reshape(RB // 8, 8, LANES) * invb[k][None]
            racc[rows, :] = acc.reshape(RB, LANES)
            return carry

        lax.fori_loop(0, ROWS // RB, step, 0)

    def row_send(it):
        for t in range(8):
            rowr[it, my_slot, t : t + 1, :] = jnp.sum(
                racc[t * LANES : (t + 1) * LANES, :].T, axis=0, keepdims=True
            )
        mine = rowr.at[it, my_slot]
        for j in range(1, NP):
            rcopy(mine, mine, r_send, r_recv.at[it], r, (p + j) % NP).start()

    def row_wait(it):
        theirs = rowr.at[it, pl.ds(0, NP - 1)]
        rcopy(theirs, theirs, r_send, r_recv.at[it], r, p).wait_recv()
        total = rowr[it, 0]
        for j in range(1, NP):
            total = total + rowr[it, j]
        weights = 1.0 / total
        for t in range(8):
            wexp[t * LANES : (t + 1) * LANES, :] = jnp.broadcast_to(
                weights[t : t + 1, :], (LANES, LANES)
            ).T

    def column_pass(it, ch):
        def step(g, accs):
            rows = pl.ds(pl.multiple_of(g * 128, 128), 128)
            w = wexp[rows, :].reshape(16, 8, LANES)
            return tuple(
                accs[t] + jnp.sum(exps[ch * CT + t, rows, :].reshape(16, 8, LANES) * w, axis=0)
                for t in range(CT)
            )

        accs = lax.fori_loop(
            0, ROWS // 128, step, tuple(jnp.zeros((8, LANES), jnp.float32) for _ in range(CT))
        )
        for t in range(CT):
            k = ch * CT + t
            colr[it, r, k : k + 1, :] = jnp.sum(accs[t], axis=0, keepdims=True)
        column_send(it, ch)

    def owner_send(kind, acc, buf, dy):
        ys = (y + dy) % Y
        for t in range(2):
            block = acc[pl.ds(pl.multiple_of(ys * PLANE + t * LANES, LANES), LANES), :]
            buf[ys, my_slot, t : t + 1, :] = jnp.sum(block.T, axis=0, keepdims=True)
        mine = buf.at[ys, my_slot]
        for dx in (0, 1):
            for dc in (0, 1):
                if (dy, dx, dc) == (0, 0, 0):
                    continue
                q = pidx(ys, (x + dx) % 2, (c + dc) % 2)
                rcopy(mine, mine, t_send.at[kind], t_recv.at[kind], r, q).start()

    def owner_total(kind, buf):
        theirs = buf.at[y, pl.ds(0, NP - 1)]
        rcopy(theirs, theirs, t_send.at[kind], t_recv.at[kind], r, p).wait_recv()
        total = buf[y, 0]
        for j in range(1, NP):
            total = total + buf[y, j]
        for t in range(2):
            own_buf[kind, t * LANES : (t + 1) * LANES, :] = jnp.broadcast_to(
                total[t : t + 1, :], (LANES, LANES)
            ).T
        return own_buf[kind, pl.ds(pl.multiple_of(c * LANES + x * OWN, OWN), OWN), :]

    def pair_copy(kind, g, px, dy):
        ys = (y + dy) % Y
        rows = pl.ds(pl.multiple_of(ys * PLANE + pc * LANES, LANES), LANES)
        return rcopy(g.at[rows], px.at[ys], p_send.at[kind], p_recv.at[kind, dy], r, partner)

    def scatter_send(kind, g, px, ps, rs, dy):
        ys = (y + dy) % Y
        block = px.at[ys]
        rcopy(block, block, p_send.at[kind], p_recv.at[kind, dy], r, partner).wait_recv()
        rows = pl.ds(pl.multiple_of(ys * PLANE + c * LANES, LANES), LANES)
        ps[ys] = g[rows, :] + px[ys]
        for dx in (0, 1):
            if (dy, dx) == (0, 0):
                continue
            xs = (x + dx) % 2
            src = ps.at[ys, pl.ds(pl.multiple_of(xs * OWN, OWN), OWN)]
            rcopy(src, rs.at[y * 2 + x], s_send.at[kind], s_recv.at[kind],
                  r, pidx(ys, xs, c)).start()

    def scatter_total(kind, ps, rs):
        theirs = rs.at[pl.ds(0, 7)]
        rcopy(theirs, theirs, s_send.at[kind], s_recv.at[kind], r, partner).wait_recv()
        total = ps[y, pl.ds(pl.multiple_of(x * OWN, OWN), OWN), :]
        for dy, dx in peers:
            total = total + rs[((y + dy) % Y) * 2 + (x + dx) % 2]
        return total

    far_first = (2, 1, 3, 0)

    with scope("student"):
        student_piece(far_first[0])
    for ch in range(NCH):
        with scope("column_wait"):
            column_wait(0, ch)
        with scope("row_pass"):
            row_pass(ch)
    with scope("row_send"):
        row_send(0)
    with scope("student"):
        student_piece(far_first[1])
        student_piece(far_first[2])
    with scope("row_wait"):
        row_wait(0)
    for ch in range(NCH):
        with scope("column_pass"):
            column_pass(1, ch)
        if ch < 3:
            with scope("scatter_a"):
                scatter_send(0, ga, pxa, psa, rsa, far_first[ch])
    with scope("student"):
        student_piece(far_first[3])
    for ch in range(NCH):
        with scope("column_wait"):
            column_wait(1, ch)
        with scope("row_pass"):
            row_pass(ch)
        if ch == 0:
            with scope("scatter_a"):
                scatter_send(0, ga, pxa, psa, rsa, far_first[3])
    with scope("row_send"):
        row_send(1)
    with scope("owner_a"):
        for dy in far_first:
            owner_send(0, sacc, tota, dy)
    with scope("row_wait"):
        row_wait(1)
    for ch in range(NCH):
        with scope("column_pass"):
            column_pass(2, ch)

    with scope("student_own"):
        sample_total = owner_total(0, tota)
        first = scatter_total(0, psa, rsa)
        inv_sample = 1.0 / sample_total
        ownd[...] = first * jnp.concatenate([inv_sample, inv_sample], axis=1)
        owns[...] = jnp.log(sample_total)

    with scope("column_wait"):
        for ch in range(NCH):
            column_wait(2, ch)
    for i, dy in enumerate(far_first):
        with scope("final_plane"):
            ys = (y + dy) % Y
            rows = pl.ds(pl.multiple_of(ys * PLANE, PLANE), PLANE)
            total = jnp.zeros((PLANE, LANES), jnp.float32)
            parts = []
            for k in range(KT):
                part = exps[k, rows, :].reshape(PLANE // 8, 8, LANES) * invb[k][None]
                part = part.reshape(PLANE, LANES)
                total = total + part
                parts.append(part.astype(jnp.bfloat16))
            racc[rows, :] = total
            gb[rows, :] = lax.dot_general(
                jnp.concatenate(parts, axis=1), half[...], NT,
                preferred_element_type=jnp.float32,
            )
        pair_copy(1, gb, pxb, dy).start()
        with scope("owner_b"):
            owner_send(1, racc, totb, dy)
        if i > 0:
            with scope("scatter_b"):
                scatter_send(1, gb, pxb, psb, rsb, far_first[i - 1])
    with scope("scatter_last"):
        scatter_send(1, gb, pxb, psb, rsb, far_first[3])

    floats = stu[my_slot].astype(jnp.float32)
    norm = jnp.sqrt(jnp.sum(floats * floats, axis=1, keepdims=True) + EPSILON)
    own = floats / norm
    half_own = own.astype(jnp.bfloat16).astype(jnp.float32)
    with scope("row_total"):
        weight = 1.0 / owner_total(1, totb)
    with scope("last_wait"):
        second = scatter_total(1, psb, rsb)
    with scope("finish"):
        pulled = second * jnp.concatenate([weight, weight], axis=1)
        direction = (ownd[...] - pulled) / STUDENT_TEMP
        cross = jnp.sum(half_own * pulled, axis=1, keepdims=True) / STUDENT_TEMP
        radial = jnp.sum(own * direction, axis=1, keepdims=True)
        grad_ref[...] = (direction - own * radial) / norm
        loss_ref[...] = owns[...] - jnp.broadcast_to(cross, (OWN, LANES))

    def sent(ref, sem):
        rcopy(ref, ref, sem, sem, r, partner).wait_send()

    with scope("sent"):
        sent(tea.at[pl.ds(0, 15)], g_send.at[0])
        sent(stu.at[pl.ds(0, 15)], g_send.at[1])
        sent(colr.at[:, pl.ds(0, R - 1)], c_send)
        sent(rowr.at[:, pl.ds(0, NP - 1)], r_send)
        for kind, (tot, px, rs) in enumerate(((tota, pxa, rsa), (totb, pxb, rsb))):
            sent(tot.at[0, pl.ds(0, NP - 1)], t_send.at[kind])
            sent(px, p_send.at[kind])
            sent(rs.at[pl.ds(0, 7)], s_send.at[kind])


def on_device(teacher_rows, student_rows, prototypes):
    f32, bf16 = jnp.float32, jnp.bfloat16
    vmem = lambda shape, dtype=f32: pltpu.VMEM(shape, dtype)
    dma = lambda *shape: pltpu.SemaphoreType.DMA(shape)
    grads, loss = pl.pallas_call(
        kernel,
        out_shape=(
            jax.ShapeDtypeStruct((OWN, D), f32),
            jax.ShapeDtypeStruct((OWN, LANES), f32),
        ),
        in_specs=[pl.BlockSpec(memory_space=pl.ANY)] * 3,
        out_specs=(pl.BlockSpec(memory_space=pltpu.VMEM), pl.BlockSpec(memory_space=pltpu.VMEM)),
        scratch_shapes=[
            vmem((KT, ROWS, LANES)),
            vmem((D, K), bf16), vmem((D, K), bf16),
            vmem((NP, OWN, D), bf16), vmem((NP, OWN, D), bf16),
            vmem((ROWS, D), bf16),
            vmem((ROWS, LANES)), vmem((ROWS, LANES)),
            vmem((ROWS, LANES)), vmem((ROWS, LANES)),
            vmem((2, PLANE, LANES)),
            vmem((8, K)), vmem((KT, 8, LANES)), vmem((KT, 8, LANES)),
            vmem((ITERS, R, KT, LANES)),
            vmem((2, NP, 8, LANES)),
            vmem((ROWS, D)), vmem((ROWS, D)),
            vmem((Y, LANES, D)), vmem((Y, LANES, D)),
            vmem((Y, LANES, D)), vmem((Y, LANES, D)),
            vmem((8, OWN, D)), vmem((8, OWN, D)),
            vmem((Y, NP, 2, LANES)), vmem((Y, NP, 2, LANES)),
            vmem((OWN, D)), vmem((OWN, LANES)),
            dma(3),
            dma(2), dma(2, 2, Y),
            pltpu.SemaphoreType.DMA, dma(ITERS, NCH),
            pltpu.SemaphoreType.DMA, dma(2),
            dma(2), dma(2),
            dma(2), dma(2, Y),
            dma(2), dma(2),
        ],
        compiler_params=pltpu.CompilerParams(
            collective_id=0, has_side_effects=True, vmem_limit_bytes=67043328
        ),
        name="prototype_head",
    )(teacher_rows, student_rows, prototypes)
    return grads, loss[:, 0]


def solution(mesh):
    in_specs = (P(("rows", "protos"), None), P(("rows", "protos"), None), P(None, "protos"))
    out_specs = (P(("rows", "protos"), None), P(("rows", "protos")))
    return jax.shard_map(
        on_device, mesh=mesh, in_specs=in_specs, out_specs=out_specs, check_vma=False
    )
```

time: 98.7 us -> 77.7 us (0.79)
  Pallas kernels: 95 us -> 74 us
    pallas_call x1, Pallas kernels: 95 us -> 74 us  [on_device(): pl.pallas_call(kernel, out_shape=(jax.ShapeDtypeStruct((OWN, D), f32), ja...]
where the time goes in v2:
time: 77.7 us; the launch traced here: 77.5 us
  Pallas kernels  74 us (95%)
  local copies, waits for them, and re-layouts  2.86 us (4%)
    pallas_call x1, Pallas kernels, on_device(): pl.pallas_call(kernel, out_shape=(jax.ShapeDtypeStruct((OWN, D), f32), ja...  74 us

profile of v2, /device:TPU:1, one launch (start us, length us, event | category | flops | bytes accessed | tf_op | source)
XLA Modules:
  0.0 77.5 jit_solution(7222898489244391844)
XLA Ops:
  0.6 74.0 %prototype_head.1 = (f32[64,256]{1,0:T(8,128)}, f32[64,128]{1,0:T(8,128)}) custom-call(bf16[64,256]{1,0:T(8,128)(2,1)} %tea_hbm.1, bf16[64,256]{1,0:T(8,128)(2,1)} %stu_hbm.1, bf16[256,8192]{1,0:T(8,128)(2,1)} %pro_hbm.1), custom_call_target="tpu_custom_call" | custom-call | tf_op jit(solution)/shard_map/prototype_head/pallas_call | solution.py:430
  74.7 1.4 %slice_reduce_fusion = f32[64]{0:T(128)} fusion(f32[64,128]{1,0:T(8,128)} %get-tuple-element.5), kind=kLoop, calls=%fused_computation | loop fusion | bytes 512 | tf_op jit(solution)/shard_map/slice | solution.py:468
  76.0 1.5 %copy.6 = f32[64,256]{1,0:T(8,128)} copy(f32[64,256]{1,0:T(8,128)} %get-tuple-element.8) | data formatting | bytes 131072

commit v3 on v2

--- a/solution.py
+++ b/solution.py
@@ -27,6 +27,7 @@
 CW = K // NCH
 CT = CW // LANES
 RB = 256
+FB = 64
 KT = K // LANES
 MESH = pl.DeviceIdType.MESH
 scope = lambda name: contextlib.nullcontext()
@@ -35,13 +36,13 @@
 
 def kernel(
     tea_hbm, stu_hbm, pro_hbm,
-    grad_ref, loss_ref,
+    out_ref,
     exps, proto, half, tea, stu, unit,
     tscale, wexp, racc, sacc, own_buf,
-    rnorm, invb, colp, colr, rowr,
-    ga, gb, pxa, pxb, psa, psb, rsa, rsb, tota, totb, ownd, owns,
+    rnorm, invb, colp, colf, colr, rowr,
+    ga, gb, pxa, pxb, psa, psb, rsa, rsb, fwa, fwb, tota, totb, ownd, owns,
     load_sem, g_send, g_recv, c_send, c_recv, r_send, r_recv,
-    t_send, t_recv, p_send, p_recv, s_send, s_recv,
+    t_send, t_recv, p_send, p_recv, s_send, s_recv, f_recv,
 ):
     r = lax.axis_index("rows")
     p = lax.axis_index("protos")
@@ -54,6 +55,7 @@
     def slot(yy, xx, cc):
         return yy * 4 + cc * 2 + xx
 
+    apart = pl.when(p >= 0)
     partner = pidx(y, x, pc)
     my_slot = slot(y, x, c)
 
@@ -125,6 +127,7 @@
 
     def column_send(it, ch):
         piece = pl.ds(ch * CT, CT)
+        colr[it, r, piece] = colf[piece, :].astype(jnp.bfloat16)
         mine = colr.at[it, r, piece]
         for j in range(1, R):
             rcopy(mine, mine, c_send, c_recv.at[it, ch], (r + j) % R, p).start()
@@ -133,9 +136,9 @@
         piece = pl.ds(ch * CT, CT)
         theirs = colr.at[it, pl.ds(0, R - 1), piece]
         rcopy(theirs, theirs, c_send, c_recv.at[it, ch], r, p).wait_recv()
-        total = colr[it, 0, piece]
+        total = colr[it, 0, piece].astype(jnp.float32)
         for j in range(1, R):
-            total = total + colr[it, j, piece]
+            total = total + colr[it, j, piece].astype(jnp.float32)
         inverse = 1.0 / total
         for t in range(CT):
             invb[ch * CT + t] = jnp.broadcast_to(inverse[t : t + 1, :], (8, LANES))
@@ -144,7 +147,8 @@
 
     def exp_tiles(rows, block, first, k0, k1):
         dots = jnp.dot(
-            block, proto[:, k0 * LANES : k1 * LANES], preferred_element_type=jnp.float32
+            block[...].reshape(PLANE, D), proto[:, k0 * LANES : k1 * LANES],
+            preferred_element_type=jnp.float32,
         )
         row_scale = tscale[rows, :].reshape(PLANE // 8, 8, LANES)
         for k in range(k0, k1):
@@ -167,19 +171,19 @@
         with scope("exp_plane"):
             ys = (y + order[s]) % Y
             rows = pl.ds(pl.multiple_of(ys * PLANE, PLANE), PLANE)
-            block = tea[pl.ds(ys * 4, 4)].reshape(PLANE, D)
-            wide = block.astype(jnp.float32)
+            block = tea.at[pl.ds(ys * 4, 4)]
+            wide = block[...].reshape(PLANE, D).astype(jnp.float32)
             total = jnp.sum(wide * wide, axis=1, keepdims=True)
             scale = (LOG2E / TEACHER_TEMP) / jnp.sqrt(total + EPSILON)
             tscale[rows, :] = jnp.broadcast_to(scale, (PLANE, LANES))
             if s < 3:
-                exp_tiles(rows, block, s == 0, 0, KT)
+                apart(lambda: exp_tiles(rows, block, s == 0, 0, KT))
             else:
                 for h in range(2):
-                    exp_tiles(rows, block, False, h * KT // 2, (h + 1) * KT // 2)
+                    apart(lambda: exp_tiles(rows, block, False, h * KT // 2, (h + 1) * KT // 2))
                     for ch in range(h * NCH // 2, (h + 1) * NCH // 2):
                         for k in range(ch * CT, (ch + 1) * CT):
-                            colr[0, r, k : k + 1, :] = jnp.sum(colp[k], axis=0, keepdims=True)
+                            colf[k : k + 1, :] = jnp.sum(colp[k], axis=0, keepdims=True)
                         column_send(0, ch)
 
     with scope("student_rows"):
@@ -201,15 +205,19 @@
     def student_piece(dy):
         ys = (y + dy) % Y
         rows = pl.ds(pl.multiple_of(ys * PLANE, PLANE), PLANE)
-        logits = jnp.dot(unit[rows, :], half[...], preferred_element_type=jnp.float32)
-        value = jnp.exp2(logits * (LOG2E / STUDENT_TEMP))
-        total = value[:, :LANES]
-        for k in range(1, KT):
-            total = total + value[:, k * LANES : (k + 1) * LANES]
-        sacc[rows, :] = total
-        ga[rows, :] = lax.dot_general(
-            value.astype(jnp.bfloat16), half[...], NT, preferred_element_type=jnp.float32
-        )
+
+        @apart
+        def _():
+            logits = jnp.dot(unit[rows, :], half[...], preferred_element_type=jnp.float32)
+            value = jnp.exp2(logits * (LOG2E / STUDENT_TEMP))
+            total = value[:, :LANES]
+            for k in range(1, KT):
+                total = total + value[:, k * LANES : (k + 1) * LANES]
+            sacc[rows, :] = total
+            ga[rows, :] = lax.dot_general(
+                value.astype(jnp.bfloat16), half[...], NT, preferred_element_type=jnp.float32
+            )
+
         pair_copy(0, ga, pxa, dy).start()
 
     def row_pass(ch):
@@ -260,7 +268,7 @@
         )
         for t in range(CT):
             k = ch * CT + t
-            colr[it, r, k : k + 1, :] = jnp.sum(accs[t], axis=0, keepdims=True)
+            colf[k : k + 1, :] = jnp.sum(accs[t], axis=0, keepdims=True)
         column_send(it, ch)
 
     def owner_send(kind, acc, buf, dy):
@@ -293,28 +301,41 @@
         rows = pl.ds(pl.multiple_of(ys * PLANE + pc * LANES, LANES), LANES)
         return rcopy(g.at[rows], px.at[ys], p_send.at[kind], p_recv.at[kind, dy], r, partner)
 
-    def scatter_send(kind, g, px, ps, rs, dy):
+    def scatter_send(kind, dy):
+        g, px, ps, rs, fw = products[kind]
         ys = (y + dy) % Y
         block = px.at[ys]
         rcopy(block, block, p_send.at[kind], p_recv.at[kind, dy], r, partner).wait_recv()
         rows = pl.ds(pl.multiple_of(ys * PLANE + c * LANES, LANES), LANES)
         ps[ys] = g[rows, :] + px[ys]
+        part = [pl.ds(pl.multiple_of((x + dx) % 2 * OWN, OWN), OWN) for dx in (0, 1)]
+        if dy == 2:
+            for dx, side in ((0, 3), (1, 1)):
+                rcopy(ps.at[ys, part[dx]], fw.at[dx], s_send.at[kind], f_recv.at[kind, dx],
+                      r, pidx((y + side) % Y, x, c)).start()
+            return
+        if dy in (1, 3):
+            dx = 1 if dy == 1 else 0
+            rcopy(fw.at[dx], fw.at[dx], s_send.at[kind], f_recv.at[kind, dx],
+                  r, partner).wait_recv()
+            ps[ys, part[dx], :] = ps[ys, part[dx], :] + fw[dx]
         for dx in (0, 1):
-            if (dy, dx) == (0, 0):
-                continue
-            xs = (x + dx) % 2
-            src = ps.at[ys, pl.ds(pl.multiple_of(xs * OWN, OWN), OWN)]
-            rcopy(src, rs.at[y * 2 + x], s_send.at[kind], s_recv.at[kind],
-                  r, pidx(ys, xs, c)).start()
-
-    def scatter_total(kind, ps, rs):
-        theirs = rs.at[pl.ds(0, 7)]
+            if (dy, dx) != (0, 0):
+                rcopy(ps.at[ys, part[dx]], rs.at[y * 2 + x], s_send.at[kind], s_recv.at[kind],
+                      r, pidx(ys, (x + dx) % 2, c)).start()
+
+    def scatter_total(kind):
+        g, px, ps, rs, fw = products[kind]
+        theirs = rs.at[pl.ds(0, 5)]
         rcopy(theirs, theirs, s_send.at[kind], s_recv.at[kind], r, partner).wait_recv()
-        total = ps[y, pl.ds(pl.multiple_of(x * OWN, OWN), OWN), :]
+        rows = pl.ds(pl.multiple_of(my_slot * OWN, OWN), OWN)
+        total = g[rows, :] + px[y, pl.ds(pl.multiple_of(x * OWN, OWN), OWN), :]
         for dy, dx in peers:
-            total = total + rs[((y + dy) % Y) * 2 + (x + dx) % 2]
+            if dy != 2:
+                total = total + rs[((y + dy) % Y) * 2 + (x + dx) % 2]
         return total
 
+    products = ((ga, pxa, psa, rsa, fwa), (gb, pxb, psb, rsb, fwb))
     far_first = (2, 1, 3, 0)
 
     with scope("student"):
@@ -322,6 +343,9 @@
     for ch in range(NCH):
         with scope("column_wait"):
             column_wait(0, ch)
+        if ch == 1:
+            with scope("scatter_a"):
+                scatter_send(0, far_first[0])
         with scope("row_pass"):
             row_pass(ch)
     with scope("row_send"):
@@ -331,22 +355,22 @@
         student_piece(far_first[2])
     with scope("row_wait"):
         row_wait(0)
+    with scope("scatter_a"):
+        scatter_send(0, far_first[1])
+        scatter_send(0, far_first[2])
     for ch in range(NCH):
         with scope("column_pass"):
             column_pass(1, ch)
-        if ch < 3:
-            with scope("scatter_a"):
-                scatter_send(0, ga, pxa, psa, rsa, far_first[ch])
     with scope("student"):
         student_piece(far_first[3])
     for ch in range(NCH):
         with scope("column_wait"):
             column_wait(1, ch)
+        if ch == 1:
+            with scope("scatter_a"):
+                scatter_send(0, far_first[3])
         with scope("row_pass"):
             row_pass(ch)
-        if ch == 0:
-            with scope("scatter_a"):
-                scatter_send(0, ga, pxa, psa, rsa, far_first[3])
     with scope("row_send"):
         row_send(1)
     with scope("owner_a"):
@@ -358,40 +382,55 @@
         with scope("column_pass"):
             column_pass(2, ch)
 
+    def final_scale(row0, ch0, ch1):
+        for g in range(PLANE // FB):
+            rows = pl.ds(pl.multiple_of(row0 + g * FB, FB), FB)
+            total = jnp.zeros((FB, LANES), jnp.float32) if ch0 == 0 else racc[rows, :]
+            for k in range(ch0 * CT, ch1 * CT):
+                part = exps[k, rows, :].reshape(FB // 8, 8, LANES) * invb[k][None]
+                part = part.reshape(FB, LANES)
+                total = total + part
+                proto[g * FB : (g + 1) * FB, k * LANES : (k + 1) * LANES] = part.astype(
+                    jnp.bfloat16
+                )
+            racc[rows, :] = total
+
     with scope("student_own"):
         sample_total = owner_total(0, tota)
-        first = scatter_total(0, psa, rsa)
+        first = scatter_total(0)
         inv_sample = 1.0 / sample_total
         ownd[...] = first * jnp.concatenate([inv_sample, inv_sample], axis=1)
         owns[...] = jnp.log(sample_total)
 
-    with scope("column_wait"):
-        for ch in range(NCH):
-            column_wait(2, ch)
-    for i, dy in enumerate(far_first):
+    last_order = (2, 1, 3, 0)
+    for i, dy in enumerate(last_order):
+        ys = (y + dy) % Y
+        row0 = pl.multiple_of(ys * PLANE, PLANE)
+        if i == 0:
+            for ch in range(NCH):
+                with scope("column_wait"):
+                    column_wait(2, ch)
+                with scope("final_scale"):
+                    final_scale(row0, ch, ch + 1)
         with scope("final_plane"):
-            ys = (y + dy) % Y
-            rows = pl.ds(pl.multiple_of(ys * PLANE, PLANE), PLANE)
-            total = jnp.zeros((PLANE, LANES), jnp.float32)
-            parts = []
-            for k in range(KT):
-                part = exps[k, rows, :].reshape(PLANE // 8, 8, LANES) * invb[k][None]
-                part = part.reshape(PLANE, LANES)
-                total = total + part
-                parts.append(part.astype(jnp.bfloat16))
-            racc[rows, :] = total
-            gb[rows, :] = lax.dot_general(
-                jnp.concatenate(parts, axis=1), half[...], NT,
-                preferred_element_type=jnp.float32,
-            )
+            @apart
+            def _():
+                if i > 0:
+                    final_scale(row0, 0, NCH)
+                gb[pl.ds(row0, PLANE), :] = lax.dot_general(
+                    proto[...], half[...], NT, preferred_element_type=jnp.float32
+                )
         pair_copy(1, gb, pxb, dy).start()
         with scope("owner_b"):
             owner_send(1, racc, totb, dy)
-        if i > 0:
+        if i == 1:
             with scope("scatter_b"):
-                scatter_send(1, gb, pxb, psb, rsb, far_first[i - 1])
+                scatter_send(1, last_order[0])
+    with scope("scatter_b"):
+        scatter_send(1, last_order[1])
+        scatter_send(1, last_order[2])
     with scope("scatter_last"):
-        scatter_send(1, gb, pxb, psb, rsb, far_first[3])
+        scatter_send(1, last_order[3])
 
     floats = stu[my_slot].astype(jnp.float32)
     norm = jnp.sqrt(jnp.sum(floats * floats, axis=1, keepdims=True) + EPSILON)
@@ -400,14 +439,14 @@
     with scope("row_total"):
         weight = 1.0 / owner_total(1, totb)
     with scope("last_wait"):
-        second = scatter_total(1, psb, rsb)
+        second = scatter_total(1)
     with scope("finish"):
         pulled = second * jnp.concatenate([weight, weight], axis=1)
         direction = (ownd[...] - pulled) / STUDENT_TEMP
         cross = jnp.sum(half_own * pulled, axis=1, keepdims=True) / STUDENT_TEMP
         radial = jnp.sum(own * direction, axis=1, keepdims=True)
-        grad_ref[...] = (direction - own * radial) / norm
-        loss_ref[...] = owns[...] - jnp.broadcast_to(cross, (OWN, LANES))
+        out_ref[:, :D] = (direction - own * radial) / norm
+        out_ref[:, D:] = owns[...] - jnp.broadcast_to(cross, (OWN, LANES))
 
     def sent(ref, sem):
         rcopy(ref, ref, sem, sem, r, partner).wait_send()
@@ -427,14 +466,11 @@
     f32, bf16 = jnp.float32, jnp.bfloat16
     vmem = lambda shape, dtype=f32: pltpu.VMEM(shape, dtype)
     dma = lambda *shape: pltpu.SemaphoreType.DMA(shape)
-    grads, loss = pl.pallas_call(
+    out = pl.pallas_call(
         kernel,
-        out_shape=(
-            jax.ShapeDtypeStruct((OWN, D), f32),
-            jax.ShapeDtypeStruct((OWN, LANES), f32),
-        ),
+        out_shape=jax.ShapeDtypeStruct((OWN, D + LANES), f32),
         in_specs=[pl.BlockSpec(memory_space=pl.ANY)] * 3,
-        out_specs=(pl.BlockSpec(memory_space=pltpu.VMEM), pl.BlockSpec(memory_space=pltpu.VMEM)),
+        out_specs=pl.BlockSpec(memory_space=pltpu.VMEM),
         scratch_shapes=[
             vmem((KT, ROWS, LANES)),
             vmem((D, K), bf16), vmem((D, K), bf16),
@@ -444,12 +480,13 @@
             vmem((ROWS, LANES)), vmem((ROWS, LANES)),
             vmem((2, PLANE, LANES)),
             vmem((8, K)), vmem((KT, 8, LANES)), vmem((KT, 8, LANES)),
-            vmem((ITERS, R, KT, LANES)),
+            vmem((KT, LANES)), vmem((ITERS, R, KT, LANES), bf16),
             vmem((2, NP, 8, LANES)),
             vmem((ROWS, D)), vmem((ROWS, D)),
             vmem((Y, LANES, D)), vmem((Y, LANES, D)),
             vmem((Y, LANES, D)), vmem((Y, LANES, D)),
             vmem((8, OWN, D)), vmem((8, OWN, D)),
+            vmem((2, OWN, D)), vmem((2, OWN, D)),
             vmem((Y, NP, 2, LANES)), vmem((Y, NP, 2, LANES)),
             vmem((OWN, D)), vmem((OWN, LANES)),
             dma(3),
@@ -458,14 +495,14 @@
             pltpu.SemaphoreType.DMA, dma(2),
             dma(2), dma(2),
             dma(2), dma(2, Y),
-            dma(2), dma(2),
+            dma(2), dma(2), dma(2, 2),
         ],
         compiler_params=pltpu.CompilerParams(
             collective_id=0, has_side_effects=True, vmem_limit_bytes=67043328
         ),
         name="prototype_head",
     )(teacher_rows, student_rows, prototypes)
-    return grads, loss[:, 0]
+    return out[:, :D], out[:, D]
 
 
 def solution(mesh):

time: 77.7 us -> 72.2 us (0.929)
  Pallas kernels: 74 us -> 68 us
    pallas_call x1, Pallas kernels: 74 us -> 68 us  [on_device(): pl.pallas_call(kernel, out_shape=jax.ShapeDtypeStruct((OWN, D + LANES), f...]
    slice x1 -> x2, local copies, waits for them, and re-layouts: 1.38 us -> 2.86 us  [on_device(): return (out[:, :D], out[:, D])]
    unnamed x1 -> x0, local copies, waits for them, and re-layouts: 1.47 us -> none
where the time goes in v3:
time: 72.2 us; the launch traced here: 71.5 us
  Pallas kernels  68 us (94%)
  local copies, waits for them, and re-layouts  2.86 us (4%)
    pallas_call x1, Pallas kernels, on_device(): pl.pallas_call(kernel, out_shape=jax.ShapeDtypeStruct((OWN, D + LANES), f...  68 us
    slice x2, local copies, waits for them, and re-layouts, on_device(): return (out[:, :D], out[:, D])  2.86 us

profile of v3, /device:TPU:1, one launch (start us, length us, event | category | flops | bytes accessed | tf_op | source)
XLA Modules:
  0.0 71.5 jit_solution(574357250416973954)
XLA Ops:
  0.6 68.0 %prototype_head.1 = f32[64,384]{1,0:T(8,128)} custom-call(bf16[64,256]{1,0:T(8,128)(2,1)} %tea_hbm.1, bf16[64,256]{1,0:T(8,128)(2,1)} %stu_hbm.1, bf16[256,8192]{1,0:T(8,128)(2,1)} %pro_hbm.1), custom_call_target="tpu_custom_call" | custom-call | tf_op jit(solution)/shard_map/prototype_head/pallas_call | solution.py:469
  68.7 1.4 %slice_reduce_fusion = f32[64]{0:T(128)} fusion(f32[64,384]{1,0:T(8,128)} %prototype_head.1), kind=kLoop, calls=%fused_computation | loop fusion | bytes 512 | tf_op jit(solution)/shard_map/slice | solution.py:505
  70.0 1.5 %slice.6 = f32[64,256]{1,0:T(8,128)} slice(f32[64,384]{1,0:T(8,128)} %prototype_head.1), slice={[0:64], [0:256]} | slice | bytes 131072 | tf_op jit(solution)/shard_map/slice | solution.py:505

commit v4 on v3

--- a/solution.py
+++ b/solution.py
@@ -343,7 +343,7 @@
     for ch in range(NCH):
         with scope("column_wait"):
             column_wait(0, ch)
-        if ch == 1:
+        if ch == NCH - 1:
             with scope("scatter_a"):
                 scatter_send(0, far_first[0])
         with scope("row_pass"):
@@ -355,12 +355,12 @@
         student_piece(far_first[2])
     with scope("row_wait"):
         row_wait(0)
-    with scope("scatter_a"):
-        scatter_send(0, far_first[1])
-        scatter_send(0, far_first[2])
     for ch in range(NCH):
         with scope("column_pass"):
             column_pass(1, ch)
+        if ch in (0, 1):
+            with scope("scatter_a"):
+                scatter_send(0, far_first[1 + ch])
     with scope("student"):
         student_piece(far_first[3])
     for ch in range(NCH):

time: 72.2 us -> 71.9 us (level)
  no operation moved by 1% of the time
where the time goes in v4:
time: 71.9 us; the launch traced here: 71.2 us
  Pallas kernels  67.7 us (94%)
  local copies, waits for them, and re-layouts  2.86 us (4%)
    pallas_call x1, Pallas kernels, on_device(): pl.pallas_call(kernel, out_shape=jax.ShapeDtypeStruct((OWN, D + LANES), f...  67.7 us
    slice x2, local copies, waits for them, and re-layouts, on_device(): return (out[:, :D], out[:, D])  2.86 us

profile of v4, /device:TPU:1, one launch (start us, length us, event | category | flops | bytes accessed | tf_op | source)
XLA Modules:
  0.0 71.2 jit_solution(730421931352328283)
XLA Ops:
  0.6 67.7 %prototype_head.1 = f32[64,384]{1,0:T(8,128)} custom-call(bf16[64,256]{1,0:T(8,128)(2,1)} %tea_hbm.1, bf16[64,256]{1,0:T(8,128)(2,1)} %stu_hbm.1, bf16[256,8192]{1,0:T(8,128)(2,1)} %pro_hbm.1), custom_call_target="tpu_custom_call" | custom-call | tf_op jit(solution)/shard_map/prototype_head/pallas_call | solution.py:469
  68.3 1.4 %slice_reduce_fusion = f32[64]{0:T(128)} fusion(f32[64,384]{1,0:T(8,128)} %prototype_head.1), kind=kLoop, calls=%fused_computation | loop fusion | bytes 512 | tf_op jit(solution)/shard_map/slice | solution.py:505
  69.7 1.5 %slice.6 = f32[64,256]{1,0:T(8,128)} slice(f32[64,384]{1,0:T(8,128)} %prototype_head.1), slice={[0:64], [0:256]} | slice | bytes 131072 | tf_op jit(solution)/shard_map/slice | solution.py:505
